TPU v7x, 768 devices: a whole 4x8x12 slice. The times are simulated.
768 devices in a mesh: section: 48 (over x, z_lo, core), head: 16 (over y, z_hi).
Axes of the slice: x: 4, y: 8, z: 12 (z_hi: 2, z_lo: 6; z = z_hi * 6 + z_lo), core: 2. Of those that a mesh axis runs over, the one named last changes fastest.
Arguments:
- residual: bfloat16 [12288, 2, 4096], P(('section', 'head')), may hold values from -3 to 3
- queries: bfloat16 [2, 12288, 4096], P(None, 'section', 'head'), may hold values from -80 to 80
- new_kv: bfloat16 [2, 2, 12288, 1024], P(None, None, 'section'), may hold values from -6 to 6
- cache_kv: bfloat16 [2, 73728, 1024], P(None, 'section'), may hold values from -6 to 6
- lengths: int32 [48], replicated, may hold values from 1 to 1536, as said below
- out_weight: bfloat16 [48, 4096, 4096], P('section', 'head'), may hold values from -0.09375 to 0.09375
Outputs:
- advanced: bfloat16 [12288, 2, 4096], P(('section', 'head'))
Inputs may be any that keep to these rules, and one draw needn't show every extreme that they name: `lengths`: some section's cache holds 1536 positions while the section half the sections away holds at most 128.
All inputs are finite; a program needn't handle non-finite values.
Results may differ from a plain program's by a relative error of at most 0.013.
Values may be sent and summed in bfloat16 or wider, within the bound.
A program may use at most 64 MiB of HBM per device.

v0:
```python
import math

import jax
import jax.numpy as jnp
from jax import lax
from jax.sharding import PartitionSpec as P

QH = 32
KVH = 8
HD = 128
BLK = 128


neg_large = -1e30


def shifted(block, axis, distance):
    devices = range(lax.axis_size(axis))
    route = [((i - distance) % len(devices), i) for i in devices]
    return lax.ppermute(block, axis, route)


def attend_block(partial_state, query_rows, key_rows, value_rows, visible):
    running, denominator, numerator = partial_state
    scores = jnp.einsum(
        "grd,gkd->grk", query_rows, key_rows, preferred_element_type=jnp.float32
    ) * (1.0 / math.sqrt(HD))
    scores = jnp.where(visible, scores, neg_large)
    highest = jnp.maximum(running, jnp.max(scores, axis=-1))
    weights = jnp.where(visible, jnp.exp(scores - highest[..., None]), 0.0)
    factor = jnp.exp(running - highest)
    denominator = denominator * factor + jnp.sum(weights, axis=-1)
    rounded = weights.astype(jnp.bfloat16)
    numerator = numerator * factor[..., None] + jnp.einsum(
        "grk,gkd->grd", rounded, value_rows, preferred_element_type=jnp.float32
    )
    return (highest, denominator, numerator)


def attend_range(
    partial_state,
    query_rows,
    key_blocks,
    value_blocks,
    first_block,
    block_count,
    offset,
    length_now,
):

    def one_block(block_index, state_now):
        start_row = (first_block + block_index) * BLK
        key_rows = lax.dynamic_slice_in_dim(key_blocks, start_row, BLK, 1)
        value_rows = lax.dynamic_slice_in_dim(value_blocks, start_row, BLK, 1)
        position = offset + start_row + jnp.arange(BLK, dtype=jnp.int32)
        visible = (position < length_now)[None, None, :]
        return attend_block(state_now, query_rows, key_rows, value_rows, visible)

    return lax.fori_loop(0, block_count, one_block, partial_state)


def project_rows(block_heads, weight_rows):
    return jnp.dot(block_heads, weight_rows, preferred_element_type=jnp.float32)


def on_device(residual, queries, new_kv, cache_kv, lengths, out_weight):
    section_index = lax.axis_index("section")
    head_index = lax.axis_index("head")
    tick_count, row_count, head_width = queries.shape
    heads_here = head_width // HD
    group_size = QH // KVH
    kv_count = max(1, heads_here // group_size)
    inner_count = min(heads_here, group_size)
    kv_width = kv_count * HD
    kv_first = head_index * heads_here // group_size
    capacity = cache_kv.shape[1]
    cache_part = lax.dynamic_slice_in_dim(cache_kv, kv_first * HD, kv_width, 2)
    cache_heads = cache_part.reshape(2, capacity, kv_count, HD).transpose(0, 2, 1, 3)
    fresh = lax.dynamic_slice_in_dim(new_kv, kv_first * HD, kv_width, 3)
    fresh = fresh.reshape(tick_count, 2, row_count, kv_count, HD).transpose(0, 1, 3, 2, 4)
    query_rows = queries.reshape(tick_count, row_count, kv_count, inner_count, HD).transpose(
        2, 0, 3, 1, 4
    )
    all_rows = tick_count * inner_count * row_count
    query_rows = query_rows.reshape(kv_count, all_rows, HD)
    my_length = lengths[section_index]
    my_blocks = (my_length + BLK - 1) // BLK
    empty_state = (
        jnp.full((kv_count, all_rows), neg_large, jnp.float32),
        jnp.zeros((kv_count, all_rows), jnp.float32),
        jnp.zeros((kv_count, all_rows, HD), jnp.float32),
    )
    own_state = attend_range(
        empty_state, query_rows, cache_heads[0], cache_heads[1], 0, my_blocks, 0, my_length
    )
    tick_rows = inner_count * row_count
    running_ticks = own_state[0].reshape(kv_count, tick_count, tick_rows)
    denominator_ticks = own_state[1].reshape(kv_count, tick_count, tick_rows)
    numerator_ticks = own_state[2].reshape(kv_count, tick_count, tick_rows, HD)
    query_ticks = query_rows.reshape(kv_count, tick_count, tick_rows, HD)
    query_position = jnp.arange(tick_rows, dtype=jnp.int32) % row_count
    causal = (jnp.arange(row_count, dtype=jnp.int32)[None, :] <= query_position[:, None])[None]
    everything = jnp.ones((1, 1, row_count), jnp.bool_)
    head_blocks = []
    for tick_now in range(tick_count):
        state_now = (
            running_ticks[:, tick_now],
            denominator_ticks[:, tick_now],
            numerator_ticks[:, tick_now],
        )
        for earlier in range(tick_now + 1):
            mask_now = causal if earlier == tick_now else everything
            state_now = attend_block(
                state_now, query_ticks[:, tick_now], fresh[earlier, 0], fresh[earlier, 1], mask_now
            )
        mixed = state_now[2] / state_now[1][..., None]
        mixed = mixed.reshape(kv_count, inner_count, row_count, HD).transpose(2, 0, 1, 3)
        head_blocks.append(mixed.reshape(row_count, head_width).astype(jnp.bfloat16))
    weight_rows = out_weight[0]
    pieces = []
    for tick_now in range(tick_count):
        pieces.append(
            lax.psum_scatter(
                project_rows(head_blocks[tick_now], weight_rows).astype(jnp.bfloat16),
                "head",
                scatter_dimension=0,
                tiled=True,
            ).astype(jnp.float32)
        )
    projected = jnp.stack(pieces, axis=1)
    updated = (residual.astype(jnp.float32) + projected).astype(jnp.bfloat16)
    return shifted(updated, "section", 1)


def solution(mesh):
    placed = (
        P(("section", "head"), None, None),
        P(None, "section", "head"),
        P(None, None, "section", None),
        P(None, "section", None),
        P(),
        P("section", "head", None),
    )
    return jax.shard_map(
        on_device,
        mesh=mesh,
        in_specs=placed,
        out_specs=P(("section", "head"), None, None),
        check_vma=False,
    )
```

profile of v0, /device:TPU:1, one launch (start us, length us, event | category | flops | bytes accessed | tf_op | source)
XLA Modules:
  0.0 579.8 jit_solution(3752846031814133867)
XLA Ops:
  6.5 0.0 copy-start
  6.5 0.0 reduce-scatter.5.cloned.1.call-start
  6.5 1.4 dynamic_slice.15
  8.6 1.0 reshape.312
  9.7 1.0 dynamic-slice_bitcast_fusion
  10.7 0.0 copy-start.1
  10.7 0.2 fusion.55
  10.9 1.0 fusion.54
  12.0 1.0 fusion.56
  13.0 2.1 constant_dynamic-slice_fusion.1
  15.1 0.0 copy-done.1
  15.1 12.4 %while.14 = (s32[]{:T(128)}, f32[1,1024]{1,0:T(1,128)S(1)}, f32[1,1024]{1,0:T(1,128)S(1)}, f32[1,1024,128]{2,1,0:T(8,128)S(1)}, s32[]{:T(128)}, /*index=5*/s32[]...) while((s32[]{:T(128)}, f32[1,1024]{1,0:T(1,128)S(1)}, ...), condition=%wide.region_3.4_spmd, body=%wide.region_0.3_spmd.sunk | while | flops 68552960 | bytes 3015363 | solution.py:59
  15.1 0.6 add_compare_fusion.2
  15.8 1.0 fusion.66
  16.8 0.1 fusion.67
  17.0 1.3 fusion.68
  18.3 0.6 add_compare_fusion.2
  18.9 1.0 fusion.66
  19.9 0.1 fusion.67
  20.1 1.3 fusion.68
  21.4 0.6 add_compare_fusion.2
  22.0 1.0 fusion.66
  23.0 0.1 fusion.67
  23.2 1.3 fusion.68
  24.5 0.6 add_compare_fusion.2
  25.1 1.0 fusion.66
  26.1 0.1 fusion.67
  26.3 1.3 fusion.68
  27.6 0.0 copy-start.2
  27.6 0.6 broadcast.108
  28.2 0.7 reduce.26
  28.9 0.7 reduce.27
  29.6 0.0 copy-start.4
  29.7 0.1 fusion.27
  29.8 1.4 fusion.29
  31.2 1.1 fusion.23
  32.4 0.0 copy-done.2
  32.4 0.0 copy-done.4
  32.4 0.3 fusion.26
  32.7 0.1 copy.13
  32.8 0.0 copy-done
  32.9 2.1 convolution_convert_fusion
  34.9 0.0 copy-start.3
  34.9 0.0 reduce-scatter.5.cloned.1.call-update
  35.0 0.0 reduce-scatter.3.cloned.1.call-start
  35.0 1.0 copy-done.3
  36.0 0.3 fusion.25
  36.3 0.1 copy.12
  36.4 2.0 convolution_convert_fusion.1
  38.5 0.0 copy-start.5
  38.5 0.0 reduce-scatter.3.cloned.1.call-update
  38.5 272.0 %reduce-scatter.5.cloned.1.call-done = bf16[16,4096]{1,0:T(8,128)(2,1)} async-done(((bf16[256,4096]{1,0:T(8,128)(2,1)}), bf16[16,4096]{1,0:T(8,128)(2,1)}) %reduce-scatter.5.cloned.1.call-update) | async-done | bytes 131088 | tf_op jit(solution)/shard_map/reduce_scatter | solution.py:123
  310.5 249.5 %reduce-scatter.3.cloned.1.call-done = bf16[16,4096]{1,0:T(8,128)(2,1)} async-done(((bf16[256,4096]{1,0:T(8,128)(2,1)}), bf16[16,4096]{1,0:T(8,128)(2,1)}) %reduce-scatter.3.cloned.1.call-update) | async-done | bytes 131088 | tf_op jit(solution)/shard_map/reduce_scatter | solution.py:123
  560.0 0.0 copy-done.5
  560.0 1.1 add_convert_fusion
  561.2 7.5 %collective-permute-start = (bf16[16,2,4096]{2,0,1:T(8,128)(2,1)S(1)}, bf16[16,2,4096]{2,0,1:T(8,128)(2,1)S(1)}, u32[]{:S(2)}, u32[]{:S(2)}) collective-permute-start(bf16[16,2,4096]{2,0,1:T(8,128)(2,1)S(1)} %add_convert_fusion), channel_id=1, source_target_pairs={{752,0},{0,16},{16,32},{32,48},{48,64},{64,80},{80,96},{96,112},{1... | collective-permute-start | bytes 786440 | tf_op jit(solution)/shard_map/ppermute | solution.py:20
  568.7 3.3 collective-permute-done
  572.0 1.0 copy.14
  (24 shorter events, 0.3 us)
Async XLA Ops:
  6.5 26.3 %copy-start = (bf16[1,256,4096]{2,1,0:T(8,128)(2,1)S(1)}, bf16[1,256,4096]{2,1,0:T(8,128)(2,1)}, u32[]{:S(2)}) copy-start(bf16[1,256,4096]{2,1,0:T(8,128)(2,1)} %param.13) | copy-start | bytes 6291460
  6.5 304.0 %reduce-scatter.5.cloned.1.call-start = ((), (), s32[]{:S(2)}) async-start(), calls=%async_computation.3 | async-start | bytes 2228224 | tf_op jit(solution)/shard_map/reduce_scatter | solution.py:123
  10.7 4.4 copy-start.1
  27.6 4.8 copy-start.2
  29.6 2.8 copy-start.4
  34.9 1.0 copy-start.3
  35.0 525.1 %reduce-scatter.3.cloned.1.call-start = ((), (), s32[]{:S(2)}) async-start(), calls=%async_computation.2 | async-start | bytes 2228224 | tf_op jit(solution)/shard_map/reduce_scatter | solution.py:123
  38.5 521.6 %copy-start.5 = (bf16[16,2,4096]{2,1,0:T(2,128)(2,1)S(1)}, bf16[16,2,4096]{2,1,0:T(2,128)(2,1)}, u32[]{:S(2)}) copy-start(bf16[16,2,4096]{2,1,0:T(2,128)(2,1)} %param.8) | copy-start | bytes 786436
  561.2 10.8 %collective-permute-start = (bf16[16,2,4096]{2,0,1:T(8,128)(2,1)S(1)}, bf16[16,2,4096]{2,0,1:T(8,128)(2,1)S(1)}, u32[]{:S(2)}, u32[]{:S(2)}) collective-permute-start(bf16[16,2,4096]{2,0,1:T(8,128)(2,1)S(1)} %add_convert_fusion), channel_id=1, source_target_pairs={{752,0},{0,16},{16,32},{32,48},{48,64},{64,80},{80,96},{96,112},{1... | collective-permute-start | bytes 786440 | tf_op jit(solution)/shard_map/ppermute | solution.py:20
Sparse Core Ops, SparseCore 0:
  35.1 275.3 reduce-scatter.4
  315.6 244.3 reduce-scatter.2
where the time goes:
time: 589 us; the launch traced here: 580 us
  waiting for transfers between devices  525 us (89%)
  matrix products  17.2 us (3%)
  between operations  14.3 us (2%)
  local copies, waits for them, and re-layouts  8.4 us (1%)
  starting transfers between devices  7.57 us (1%)
  other arithmetic  7.21 us (1%)
    reduce_scatter x2, waiting for transfers between devices, on_device(): lax.psum_scatter(project_rows(head_blocks[tick_now], weight_rows).astype(...  522 us
  transfers between devices with their start and end apart: 3, of which 3 were waited for; matrix products, arithmetic and copies ran while one was open for 0% of the time, Pallas kernels for 0%

commit v1 on v0

v1 whole, which is shorter than its diff:
```python
import functools
import math

import jax
import jax.numpy as jnp
from jax import lax
from jax.experimental import pallas as pl
from jax.experimental.pallas import tpu as pltpu
from jax.sharding import PartitionSpec as P

HD = 128
KBLK = 512
NEG = -1e30
SCALE = math.log2(math.e) / math.sqrt(HD)
SPLIT = 2
SKEW = (0, 1, 4, 5)
MESH = pl.DeviceIdType.MESH


def attend_kernel(
    len_ref, q_ref, new_ref, cache_ref, o_ref, fresh, cache, m_ref, l_ref, acc_ref, fsem, csem
):
    ticks, rows, width = q_ref.shape
    here = width // HD
    key_blocks = cache.shape[0]
    length = len_ref[lax.axis_index("section")]
    column = pl.multiple_of((lax.axis_index("head") // 2) * HD, HD)
    used = (length + KBLK - 1) // KBLK

    def fresh_copy(t, i):
        return pltpu.make_async_copy(
            new_ref.at[t, i, :, pl.ds(column, HD)],
            fresh.at[i, pl.ds(t * rows, rows), :],
            fsem.at[t, i],
        )

    def cache_copy(b, i):
        return pltpu.make_async_copy(
            cache_ref.at[i, pl.ds(b * KBLK, KBLK), pl.ds(column, HD)],
            cache.at[b, i],
            csem.at[b, i],
        )

    for t in range(ticks):
        for i in range(2):
            fresh_copy(t, i).start()
    for b in range(key_blocks):
        @pl.when(b < used)
        def _(b=b):
            for i in range(2):
                cache_copy(b, i).start()
    for t in range(ticks):
        for i in range(2):
            fresh_copy(t, i).wait()

    def scores_of(t, h, keys):
        q = q_ref[t, :, h * HD:(h + 1) * HD]
        return lax.dot_general(
            q, keys, (((1,), (1,)), ((), ())), preferred_element_type=jnp.float32
        )

    for t in range(ticks):
        count = (t + 1) * rows
        row_id = lax.broadcasted_iota(jnp.int32, (rows, count), 0)
        col_id = lax.broadcasted_iota(jnp.int32, (rows, count), 1)
        seen = col_id <= row_id + t * rows
        for h in range(here):
            at = t * here + h
            s = jnp.where(seen, scores_of(t, h, fresh[0, 0:count, :]), NEG)
            m = jnp.max(s, axis=1, keepdims=True)
            p = jnp.exp2((s - m) * SCALE)
            m_ref[at] = m
            l_ref[at] = jnp.sum(p, axis=1, keepdims=True)
            acc_ref[at] = jnp.dot(
                p.astype(jnp.bfloat16), fresh[1, 0:count, :], preferred_element_type=jnp.float32
            )

    def one_block(b, carry):
        for i in range(2):
            cache_copy(b, i).wait()
        col_id = lax.broadcasted_iota(jnp.int32, (1, KBLK), 1) + b * KBLK
        seen = col_id < length
        keys = cache[b, 0]
        values = cache[b, 1]
        for t in range(ticks):
            for h in range(here):
                at = t * here + h
                s = jnp.where(seen, scores_of(t, h, keys), NEG)
                before = m_ref[at]
                m = jnp.maximum(before, jnp.max(s, axis=1, keepdims=True))
                p = jnp.exp2((s - m) * SCALE)
                factor = jnp.exp2((before - m) * SCALE)
                m_ref[at] = m
                l_ref[at] = l_ref[at] * factor + jnp.sum(p, axis=1, keepdims=True)
                acc_ref[at] = acc_ref[at] * factor + jnp.dot(
                    p.astype(jnp.bfloat16), values, preferred_element_type=jnp.float32
                )
        return carry

    lax.fori_loop(0, used, one_block, 0)
    for t in range(ticks):
        for h in range(here):
            at = t * here + h
            o_ref[t, :, h * HD:(h + 1) * HD] = (acc_ref[at] / l_ref[at]).astype(jnp.bfloat16)


def attend(queries, new_kv, cache_kv, lengths):
    ticks, rows, width = queries.shape
    here = width // HD
    capacity = cache_kv.shape[1]
    return pl.pallas_call(
        attend_kernel,
        out_shape=jax.ShapeDtypeStruct(queries.shape, jnp.bfloat16),
        in_specs=[
            pl.BlockSpec(memory_space=pltpu.SMEM),
            pl.BlockSpec(memory_space=pltpu.VMEM),
            pl.BlockSpec(memory_space=pl.ANY),
            pl.BlockSpec(memory_space=pl.ANY),
        ],
        out_specs=pl.BlockSpec(memory_space=pltpu.VMEM),
        scratch_shapes=[
            pltpu.VMEM((2, ticks * rows, HD), jnp.bfloat16),
            pltpu.VMEM((capacity // KBLK, 2, KBLK, HD), jnp.bfloat16),
            pltpu.VMEM((ticks * here, rows, 1), jnp.float32),
            pltpu.VMEM((ticks * here, rows, 1), jnp.float32),
            pltpu.VMEM((ticks * here, rows, HD), jnp.float32),
            pltpu.SemaphoreType.DMA((ticks, 2)),
            pltpu.SemaphoreType.DMA((capacity // KBLK, 2)),
        ],
        name="attend",
    )(lengths, queries, new_kv, cache_kv)


def reduce_kernel(
    sections,
    heads_count,
    heads_ref,
    w_ref,
    res_ref,
    land_ref,
    res_land,
    part,
    buf,
    ssem,
    rsem,
    zssem,
    zrsem,
    xsem,
):
    ny = heads_count // 2
    hops = ny - 1
    groups = buf.shape[2]
    ticks = heads_ref.shape[0]
    chunk = buf.shape[3]
    wide = buf.shape[4]
    own = chunk // 2
    half = w_ref.shape[1] // 2
    section = lax.axis_index("section")
    head = lax.axis_index("head")
    y = head // 2
    z = head % 2
    after = lax.rem(section + 1, sections)
    prior = lax.rem(section + sections - 1, sections)
    ring = (lax.rem(head + 2, heads_count), lax.rem(head + heads_count - 2, heads_count))

    barrier = pltpu.get_barrier_semaphore()
    for near in ring:
        pl.semaphore_signal(barrier, inc=1, device_id=(section, near), device_id_type=MESH)
    for other in range(2):
        for where in (after, prior):
            pl.semaphore_signal(
                barrier, inc=1, device_id=(where, 2 * y + other), device_id_type=MESH
            )
    pl.semaphore_wait(barrier, 6)

    res_copy = pltpu.make_async_remote_copy(
        src_ref=res_ref,
        dst_ref=res_land,
        send_sem=xsem.at[0],
        recv_sem=xsem.at[1],
        device_id=(after, head),
        device_id_type=MESH,
    )
    res_copy.start()

    def chunk_at(d, step):
        if d == 0:
            return lax.rem(y + 2 * ny - 1 - step, ny)
        return lax.rem(y + 1 + step, ny)

    def ring_copy(step, d, g):
        return pltpu.make_async_remote_copy(
            src_ref=buf.at[step, d, g],
            dst_ref=buf.at[step + 1, d, g],
            send_sem=ssem.at[step, d, g],
            recv_sem=rsem.at[step, d, g],
            device_id=(section, ring[d]),
            device_id_type=MESH,
        )

    def column_of(d, g):
        return d * half + (g % SPLIT) * wide

    def out_copy(d, g, target, source):
        t = g // SPLIT
        return pltpu.make_async_remote_copy(
            src_ref=buf.at[hops, d, g, pl.ds(target * own, own), :],
            dst_ref=land_ref.at[source, t, :, pl.ds(column_of(d, g), wide)],
            send_sem=zssem.at[d, g, target],
            recv_sem=zrsem.at[d, g, source],
            device_id=(after, 2 * y + target),
            device_id_type=MESH,
        )

    for g in range(groups):
        t = g // SPLIT
        for d in range(2):
            rows_at = pl.multiple_of(chunk_at(d, 0) * chunk, chunk)
            block = heads_ref[t, pl.ds(rows_at, chunk), :]
            column = column_of(d, g)
            buf[0, d, g] = jnp.dot(
                block, w_ref[:, column:column + wide], preferred_element_type=jnp.float32
            ).astype(jnp.bfloat16)
        if SKEW[g] == 0:
            for d in range(2):
                ring_copy(0, d, g).start()

    tile = min(512, 2 * half)

    def fill(i, carry):
        at = pl.multiple_of(i * tile, tile)
        for t in range(ticks):
            part[t, :, pl.ds(at, tile)] = jnp.dot(
                heads_ref[t], w_ref[:, pl.ds(at, tile)], preferred_element_type=jnp.float32
            ).astype(jnp.bfloat16)
        return carry

    lax.fori_loop(0, 2 * half // tile, fill, 0)

    def slot(now, carry):
        for g in range(groups):
            t = g // SPLIT
            step = now - SKEW[g]
            if SKEW[g] > 0:
                @pl.when(step == 0)
                def _(g=g):
                    for d in range(2):
                        ring_copy(0, d, g).start()

            @pl.when(jnp.logical_and(step >= 1, step <= hops))
            def _(g=g, t=t, step=step):
                for d in range(2):
                    ring_copy(step - 1, d, g).wait_recv()
                    rows_at = pl.multiple_of(chunk_at(d, step) * chunk, chunk)
                    column = column_of(d, g)
                    mine = part[t, pl.ds(rows_at, chunk), column:column + wide]
                    buf[step, d, g] = (
                        buf[step, d, g].astype(jnp.float32) + mine.astype(jnp.float32)
                    ).astype(jnp.bfloat16)

                    @pl.when(step < hops)
                    def _():
                        ring_copy(step, d, g).start()

                    @pl.when(step == hops)
                    def _():
                        for target in range(2):
                            out_copy(d, g, target, z).start()
        return carry

    lax.fori_loop(1, hops + 1 + max(SKEW), slot, 0)

    for d in range(2):
        for g in range(groups):
            for other in range(2):
                out_copy(d, g, other, other).wait_recv()
    for d in range(2):
        for g in range(groups):
            for other in range(2):
                out_copy(d, g, other, other).wait_send()

            def drain(step, carry, d=d, g=g):
                ring_copy(step, d, g).wait_send()
                return carry

            lax.fori_loop(0, hops, drain, 0)
    res_copy.wait()


def reduce_shift(heads, weight, residual, sections, heads_count):
    ticks, rows, width = heads.shape
    depth = weight.shape[1]
    ny = heads_count // 2
    hops = ny - 1
    groups = ticks * SPLIT
    chunk = rows // ny
    wide = depth // 2 // SPLIT
    any_space = pl.BlockSpec(memory_space=pl.ANY)
    vmem = pl.BlockSpec(memory_space=pltpu.VMEM)
    return pl.pallas_call(
        functools.partial(reduce_kernel, sections, heads_count),
        out_shape=(
            jax.ShapeDtypeStruct((2, ticks, chunk // 2, depth), jnp.bfloat16),
            jax.ShapeDtypeStruct(residual.shape, jnp.bfloat16),
        ),
        in_specs=[vmem, vmem, any_space],
        out_specs=(any_space, any_space),
        scratch_shapes=[
            pltpu.VMEM((ticks, rows, depth), jnp.bfloat16),
            pltpu.VMEM((hops + 1, 2, groups, chunk, wide), jnp.bfloat16),
            pltpu.SemaphoreType.DMA((hops, 2, groups)),
            pltpu.SemaphoreType.DMA((hops, 2, groups)),
            pltpu.SemaphoreType.DMA((2, groups, 2)),
            pltpu.SemaphoreType.DMA((2, groups, 2)),
            pltpu.SemaphoreType.DMA((2,)),
        ],
        compiler_params=pltpu.CompilerParams(collective_id=0, has_side_effects=True),
        name="reduce_shift",
    )(heads, weight, residual)


def on_device(residual, queries, new_kv, cache_kv, lengths, out_weight):
    sections = lax.axis_size("section")
    heads_count = lax.axis_size("head")
    heads = attend(queries, new_kv, cache_kv, lengths)
    land, moved = reduce_shift(heads, out_weight[0], residual, sections, heads_count)
    projected = land[0].astype(jnp.float32) + land[1].astype(jnp.float32)
    return (moved.astype(jnp.float32) + projected.transpose(1, 0, 2)).astype(jnp.bfloat16)


def solution(mesh):
    placed = (
        P(("section", "head"), None, None),
        P(None, "section", "head"),
        P(None, None, "section", None),
        P(None, "section", None),
        P(),
        P("section", "head", None),
    )
    return jax.shard_map(
        on_device,
        mesh=mesh,
        in_specs=placed,
        out_specs=P(("section", "head"), None, None),
        check_vma=False,
    )
```

time: 589 us -> 92.2 us (0.16); the launches traced: 580 us -> 91 us
  waiting for transfers between devices: 525 us -> 0 us
  Pallas kernels: 0 us -> 87.3 us
  matrix products: 17.2 us -> 0 us
  between operations: 14.3 us -> 0.02 us
  starting transfers between devices: 7.57 us -> 0 us
  local copies, waits for them, and re-layouts: 8.4 us -> 1.58 us
    reduce_scatter x2 -> x0, waiting for transfers between devices: 522 us -> none  [on_device(): lax.psum_scatter(project_rows(head_blocks[tick_now], weight_rows).astype(...]
    pallas_call x0 -> x2, Pallas kernels: none -> 87.3 us  [the longest x1 81.1 us: reduce_shift(): pl.pallas_call(functools.partial(reduce_kernel, sections, heads_count), o...]
    dot_general x16 -> x0, matrix products: 17.2 us -> none  [the longest x7 6.8 us: attend_block(): jnp.einsum('grk,gkd->grd', rounded, value_rows, preferred_element_type=jn...]
    ppermute x1 -> x0, starting transfers between devices: 7.52 us -> none  [shifted(): return lax.ppermute(block, axis, route)]
  transfers between devices with their start and end apart: 3 -> 0, of which waited for: 3 -> 0; matrix products, arithmetic and copies ran while one was open for 0% -> 0% of each run, Pallas kernels for 0% -> 0%
where the time goes in v1:
time: 92.2 us; the launch traced here: 91 us
  Pallas kernels  87.3 us (95%)
  other arithmetic  2.13 us (2%)
  local copies, waits for them, and re-layouts  1.58 us (2%)
    pallas_call x1, Pallas kernels, reduce_shift(): pl.pallas_call(functools.partial(reduce_kernel, sections, heads_count), o...  81.1 us
    pallas_call x1, Pallas kernels, attend(): pl.pallas_call(attend_kernel, out_shape=jax.ShapeDtypeStruct(queries.shap...  6.18 us
    convert_element_type x1, other arithmetic, on_device(): (moved.astype(jnp.float32) + projected.transpose(1, 0, 2)).astype(jnp.bfl...  2.13 us

profile of v1, /device:TPU:1, one launch (start us, length us, event | category | flops | bytes accessed | tf_op | source)
XLA Modules:
  0.0 91.0 jit_solution(4161246913452920307)
XLA Ops:
  0.0 6.2 %attend.1.heads_ref = bf16[2,256,256]{2,1,0:T(8,128)(2,1)} custom-call(s32[48]{0:T(128)} %len_ref.1, bf16[2,256,256]{2,1,0:T(8,128)(2,1)} %q_ref.1, bf16[2,2,256,1024]{3,2,1,0:T(8,128)(2,1)} %new_ref.1, bf16[2,1536,1024]{2,1,0:T(8,128)(2,1)} %cache_ref.1), custom_call_target="tpu_custom_call" | custom-call | tf_op jit(solution)/shard_map/attend/pallas_call | solution.py:111
  6.2 81.1 %reduce_shift.1 = (bf16[2,2,16,4096]{3,2,1,0:T(8,128)(2,1)}, bf16[16,2,4096]{2,1,0:T(2,128)(2,1)}) custom-call(bf16[2,256,256]{2,1,0:T(8,128)(2,1)} %attend.1.heads_ref, bf16[256,4096]{1,0:T(8,128)(2,1)} %bitcast.7, bf16[16,2,4096]{2,1,0:T(2,128)(2,1)} %res_ref.1), custom_call_target="tpu_custom_call" | custom-call | tf_op jit(solution)/shard_map/reduce_shift/pallas_call | solution.py:300
  87.3 1.6 %copy.7 = bf16[2,2,16,4096]{3,1,2,0:T(2,128)(2,1)S(1)} copy(bf16[2,2,16,4096]{3,2,1,0:T(8,128)(2,1)} %get-tuple-element.8) | data formatting | bytes 1048576 | tf_op jit(solution)/shard_map/reduce_shift/pallas_call | solution.py:300
  88.9 2.1 %fusion = bf16[16,2,4096]{2,1,0:T(2,128)(2,1)} fusion(bf16[16,2,4096]{2,1,0:T(2,128)(2,1)} %get-tuple-element.7, bf16[2,2,16,4096]{3,1,2,0:T(2,128)(2,1)S(1)} %copy.7), kind=kLoop, calls=%fused_computation.1 | loop fusion | flops 786432 | bytes 1048576 | tf_op jit(solution)/shard_map/convert_element_type | solution.py:328

commit v2 on v1

v2 whole, which is shorter than its diff:
```python
import functools
import math

import jax
import jax.numpy as jnp
from jax import lax
from jax.experimental import pallas as pl
from jax.experimental.pallas import tpu as pltpu
from jax.sharding import PartitionSpec as P

HD = 128
KBLK = 512
NEG = -1e30
SCALE = math.log2(math.e) / math.sqrt(HD)
SPLIT = 4
SKEW = (0, 0, 0, 0, 4, 4, 5, 5)
MESH = pl.DeviceIdType.MESH


def softmax_block(s, values, m_ref, l_ref, acc_ref, at):
    before = m_ref[at]
    m = jnp.maximum(before, jnp.max(s, axis=1, keepdims=True))
    p = jnp.exp2((s - m) * SCALE)
    factor = jnp.exp2((before - m) * SCALE)
    m_ref[at] = m
    l_ref[at] = l_ref[at] * factor + jnp.sum(p, axis=1, keepdims=True)
    acc_ref[at] = acc_ref[at] * factor + jnp.dot(
        p.astype(jnp.bfloat16), values, preferred_element_type=jnp.float32
    )


def scores_of(q, keys):
    return lax.dot_general(q, keys, (((1,), (1,)), ((), ())), preferred_element_type=jnp.float32)


def kv_column():
    return pl.multiple_of((lax.axis_index("head") // 2) * HD, HD)


def attend_kernel(
    len_ref, q_hbm, new_ref, cache_ref, o_ref, q_ref, fresh, cache, m_ref, l_ref, acc_ref, fsem, csem
):
    rows, width = q_ref.shape
    here = width // HD
    key_blocks = cache.shape[0]
    length = len_ref[lax.axis_index("section")]
    column = kv_column()
    used = (length + KBLK - 1) // KBLK

    def fresh_copy(i):
        return pltpu.make_async_copy(
            new_ref.at[0, i, :, pl.ds(column, HD)], fresh.at[i], fsem.at[i]
        )

    def cache_copy(b, i):
        return pltpu.make_async_copy(
            cache_ref.at[i, pl.ds(b * KBLK, KBLK), pl.ds(column, HD)],
            cache.at[b, i],
            csem.at[b, i],
        )

    q_copy = pltpu.make_async_copy(q_hbm.at[0], q_ref, fsem.at[2])
    q_copy.start()
    for i in range(2):
        fresh_copy(i).start()
    for b in range(key_blocks):
        @pl.when(b < used)
        def _(b=b):
            for i in range(2):
                cache_copy(b, i).start()
    q_copy.wait()
    for i in range(2):
        fresh_copy(i).wait()

    row_id = lax.broadcasted_iota(jnp.int32, (rows, rows), 0)
    col_id = lax.broadcasted_iota(jnp.int32, (rows, rows), 1)
    seen = col_id <= row_id
    for h in range(here):
        s = jnp.where(seen, scores_of(q_ref[:, h * HD:(h + 1) * HD], fresh[0]), NEG)
        m = jnp.max(s, axis=1, keepdims=True)
        p = jnp.exp2((s - m) * SCALE)
        m_ref[h] = m
        l_ref[h] = jnp.sum(p, axis=1, keepdims=True)
        acc_ref[h] = jnp.dot(
            p.astype(jnp.bfloat16), fresh[1], preferred_element_type=jnp.float32
        )

    def one_block(b, carry):
        for i in range(2):
            cache_copy(b, i).wait()
        seen = lax.broadcasted_iota(jnp.int32, (1, KBLK), 1) + b * KBLK < length
        for h in range(here):
            s = scores_of(q_ref[:, h * HD:(h + 1) * HD], cache[b, 0])
            softmax_block(jnp.where(seen, s, NEG), cache[b, 1], m_ref, l_ref, acc_ref, h)
        return carry

    lax.fori_loop(0, used, one_block, 0)
    for h in range(here):
        o_ref[:, h * HD:(h + 1) * HD] = (acc_ref[h] / l_ref[h]).astype(jnp.bfloat16)


def attend(queries, new_kv, cache_kv, lengths):
    ticks, rows, width = queries.shape
    here = width // HD
    blocks = cache_kv.shape[1] // KBLK
    any_space = pl.BlockSpec(memory_space=pl.ANY)
    return pl.pallas_call(
        attend_kernel,
        out_shape=jax.ShapeDtypeStruct((rows, width), jnp.bfloat16),
        in_specs=[pl.BlockSpec(memory_space=pltpu.SMEM), any_space, any_space, any_space],
        out_specs=pl.BlockSpec(memory_space=pltpu.VMEM),
        scratch_shapes=[
            pltpu.VMEM((rows, width), jnp.bfloat16),
            pltpu.VMEM((2, rows, HD), jnp.bfloat16),
            pltpu.VMEM((blocks, 2, KBLK, HD), jnp.bfloat16),
            pltpu.VMEM((here, rows, 1), jnp.float32),
            pltpu.VMEM((here, rows, 1), jnp.float32),
            pltpu.VMEM((here, rows, HD), jnp.float32),
            pltpu.SemaphoreType.DMA((3,)),
            pltpu.SemaphoreType.DMA((blocks, 2)),
        ],
        name="attend",
    )(lengths, queries, new_kv, cache_kv)


def reduce_kernel(
    sections,
    heads_count,
    len_ref,
    heads_hbm,
    w_hbm,
    q_hbm,
    new_ref,
    cache_ref,
    res_ref,
    proj_ref,
    res_land,
    heads_ref,
    w_ref,
    q_ref,
    kv,
    m_ref,
    l_ref,
    acc_ref,
    part,
    buf,
    land,
    isem,
    wsem,
    kvsem,
    ssem,
    rsem,
    zssem,
    zrsem,
    xsem,
):
    ny = heads_count // 2
    hops = ny - 1
    groups = buf.shape[2]
    ticks, rows, width = heads_ref.shape
    here = width // HD
    chunk = buf.shape[3]
    wide = buf.shape[4]
    own = chunk // 2
    half = w_ref.shape[1] // 2
    key_blocks = kv.shape[0]
    quarter = rows // 2
    section = lax.axis_index("section")
    head = lax.axis_index("head")
    y = head // 2
    z = head % 2
    after = lax.rem(section + 1, sections)
    prior = lax.rem(section + sections - 1, sections)
    ring = (lax.rem(head + 2, heads_count), lax.rem(head + heads_count - 2, heads_count))
    column = kv_column()

    def column_of(d, g):
        return d * half + (g % SPLIT) * wide

    heads_copy = pltpu.make_async_copy(heads_hbm, heads_ref.at[0], isem.at[0])
    q_copy = pltpu.make_async_copy(q_hbm.at[1], q_ref, isem.at[1])

    def w_copy(d, g):
        at = column_of(d, g)
        return pltpu.make_async_copy(
            w_hbm.at[:, at:at + wide], w_ref.at[:, at:at + wide], wsem.at[d, g]
        )

    def fresh_copy(t, i):
        return pltpu.make_async_copy(
            new_ref.at[t, i, :, pl.ds(column, HD)],
            kv.at[0, i, pl.ds(t * rows, rows), :],
            kvsem.at[0, t, i],
        )

    def cache_copy(b, i):
        return pltpu.make_async_copy(
            cache_ref.at[i, pl.ds((b - 1) * KBLK, KBLK), pl.ds(column, HD)],
            kv.at[b, i],
            kvsem.at[b, 0, i],
        )

    heads_copy.start()
    for g in range(SPLIT):
        for d in range(2):
            w_copy(d, g).start()
    q_copy.start()
    for i in range(2):
        for t in range(ticks):
            fresh_copy(t, i).start()
        for b in range(1, key_blocks):
            cache_copy(b, i).start()

    barrier = pltpu.get_barrier_semaphore()
    for near in ring:
        pl.semaphore_signal(barrier, inc=1, device_id=(section, near), device_id_type=MESH)
    for other in range(2):
        for where in (after, prior):
            pl.semaphore_signal(
                barrier, inc=1, device_id=(where, 2 * y + other), device_id_type=MESH
            )

    def chunk_at(d, step):
        if d == 0:
            return lax.rem(y + 2 * ny - 1 - step, ny)
        return lax.rem(y + 1 + step, ny)

    def chunk_rows(d, step):
        return pl.ds(pl.multiple_of(chunk_at(d, step) * chunk, chunk), chunk)

    def ring_copy(step, d, g):
        return pltpu.make_async_remote_copy(
            src_ref=buf.at[step, d, g],
            dst_ref=buf.at[step + 1, d, g],
            send_sem=ssem.at[step, d, g],
            recv_sem=rsem.at[step, d, g],
            device_id=(section, ring[d]),
            device_id_type=MESH,
        )

    def out_copy(d, g, target, source):
        return pltpu.make_async_remote_copy(
            src_ref=buf.at[hops, d, g, pl.ds(target * own, own), :],
            dst_ref=land.at[source, d, g],
            send_sem=zssem.at[d, g, target],
            recv_sem=zrsem.at[d, g, source],
            device_id=(after, 2 * y + target),
            device_id_type=MESH,
        )

    def first_block(d, g):
        at = column_of(d, g)
        w_copy(d, g).wait()
        buf[0, d, g] = jnp.dot(
            heads_ref[0, chunk_rows(d, 0), :],
            w_ref[:, at:at + wide],
            preferred_element_type=jnp.float32,
        ).astype(jnp.bfloat16)

    heads_copy.wait()
    for d in range(2):
        first_block(d, 0)
    pl.semaphore_wait(barrier, 6)
    for d in range(2):
        ring_copy(0, d, 0).start()
    for g in range(1, SPLIT):
        for d in range(2):
            first_block(d, g)
            ring_copy(0, d, g).start()
    res_copy = pltpu.make_async_remote_copy(
        src_ref=res_ref,
        dst_ref=res_land,
        send_sem=xsem.at[0],
        recv_sem=xsem.at[1],
        device_id=(after, head),
        device_id_type=MESH,
    )
    res_copy.start()

    tile = min(512, 2 * half)

    def fill(t):
        def one(i, carry):
            at = pl.multiple_of(i * tile, tile)
            part[t, :, pl.ds(at, tile)] = jnp.dot(
                heads_ref[t], w_ref[:, pl.ds(at, tile)], preferred_element_type=jnp.float32
            ).astype(jnp.bfloat16)
            return carry

        lax.fori_loop(0, 2 * half // tile, one, 0)

    fill(0)
    m_ref[...] = jnp.full_like(m_ref, NEG)
    l_ref[...] = jnp.zeros_like(l_ref)
    acc_ref[...] = jnp.zeros_like(acc_ref)
    length = len_ref[section]
    q_copy.wait()
    for i in range(2):
        for t in range(ticks):
            fresh_copy(t, i).wait()
        for b in range(1, key_blocks):
            cache_copy(b, i).wait()

    def piece(b, at):
        h, r = at // 2, at % 2
        row_id = lax.broadcasted_iota(jnp.int32, (quarter, 1), 0) + r * quarter
        limit = jnp.where(b == 0, row_id + rows + 1, length - (b - 1) * KBLK)
        seen = lax.broadcasted_iota(jnp.int32, (quarter, KBLK), 1) < limit
        s = scores_of(q_ref[r * quarter:(r + 1) * quarter, h * HD:(h + 1) * HD], kv[b, 0])
        softmax_block(jnp.where(seen, s, NEG), kv[b, 1], m_ref, l_ref, acc_ref, at)

    def second_start(d, g):
        at = column_of(d, g)
        buf[0, d, g] = part[1, chunk_rows(d, 0), at:at + wide]
        ring_copy(0, d, g).start()

    def slot(now, carry):
        for g in range(groups):
            t = g // SPLIT
            step = now - SKEW[g]
            if SKEW[g] > key_blocks:
                @pl.when(step == 0)
                def _(g=g):
                    for d in range(2):
                        second_start(d, g)

            @pl.when(jnp.logical_and(step >= 1, step <= hops))
            def _(g=g, t=t, step=step):
                for d in range(2):
                    ring_copy(step - 1, d, g).wait_recv()
                    at = column_of(d, g)
                    mine = part[t, chunk_rows(d, step), at:at + wide]
                    buf[step, d, g] = (
                        buf[step, d, g].astype(jnp.float32) + mine.astype(jnp.float32)
                    ).astype(jnp.bfloat16)

                    @pl.when(step < hops)
                    def _():
                        ring_copy(step, d, g).start()

                    @pl.when(step == hops)
                    def _():
                        for target in range(2):
                            out_copy(d, g, target, z).start()

            if g < 2 * here:
                @pl.when(now <= key_blocks)
                def _(g=g):
                    piece(now - 1, g)

        @pl.when(now == key_blocks)
        def _():
            for at in range(2 * here):
                h, r = at // 2, at % 2
                heads_ref[1, r * quarter:(r + 1) * quarter, h * HD:(h + 1) * HD] = (
                    acc_ref[at] / l_ref[at]
                ).astype(jnp.bfloat16)
            fill(1)
            for g in range(SPLIT, groups):
                if SKEW[g] == key_blocks:
                    for d in range(2):
                        second_start(d, g)

        return carry

    lax.fori_loop(1, hops + 1 + max(SKEW), slot, 0)

    for g in range(groups):
        for d in range(2):
            for other in range(2):
                out_copy(d, g, other, other).wait_recv()
            at = column_of(d, g)
            proj_ref[g // SPLIT, :, at:at + wide] = (
                land[0, d, g].astype(jnp.float32) + land[1, d, g].astype(jnp.float32)
            ).astype(proj_ref.dtype)
    for d in range(2):
        for g in range(groups):
            for other in range(2):
                out_copy(d, g, other, other).wait_send()

            def drain(step, carry, d=d, g=g):
                ring_copy(step, d, g).wait_send()
                return carry

            lax.fori_loop(0, hops, drain, 0)
    res_copy.wait()


def reduce_shift(lengths, heads, weight, queries, new_kv, cache_kv, residual, sections, heads_count):
    ticks, rows, width = queries.shape
    here = width // HD
    depth = weight.shape[1]
    ny = heads_count // 2
    hops = ny - 1
    groups = ticks * SPLIT
    chunk = rows // ny
    wide = depth // 2 // SPLIT
    blocks = cache_kv.shape[1] // KBLK + 1
    any_space = pl.BlockSpec(memory_space=pl.ANY)
    return pl.pallas_call(
        functools.partial(reduce_kernel, sections, heads_count),
        out_shape=(
            jax.ShapeDtypeStruct((ticks, chunk // 2, depth), jnp.bfloat16),
            jax.ShapeDtypeStruct(residual.shape, jnp.bfloat16),
        ),
        in_specs=[pl.BlockSpec(memory_space=pltpu.SMEM)] + [any_space] * 6,
        out_specs=(pl.BlockSpec(memory_space=pltpu.VMEM), any_space),
        scratch_shapes=[
            pltpu.VMEM((ticks, rows, width), jnp.bfloat16),
            pltpu.VMEM(weight.shape, jnp.bfloat16),
            pltpu.VMEM((rows, width), jnp.bfloat16),
            pltpu.VMEM((blocks, 2, KBLK, HD), jnp.bfloat16),
            pltpu.VMEM((2 * here, rows // 2, 1), jnp.float32),
            pltpu.VMEM((2 * here, rows // 2, 1), jnp.float32),
            pltpu.VMEM((2 * here, rows // 2, HD), jnp.float32),
            pltpu.VMEM((ticks, rows, depth), jnp.bfloat16),
            pltpu.VMEM((hops + 1, 2, groups, chunk, wide), jnp.bfloat16),
            pltpu.VMEM((2, 2, groups, chunk // 2, wide), jnp.bfloat16),
            pltpu.SemaphoreType.DMA((2,)),
            pltpu.SemaphoreType.DMA((2, SPLIT)),
            pltpu.SemaphoreType.DMA((blocks, 2, 2)),
            pltpu.SemaphoreType.DMA((hops, 2, groups)),
            pltpu.SemaphoreType.DMA((hops, 2, groups)),
            pltpu.SemaphoreType.DMA((2, groups, 2)),
            pltpu.SemaphoreType.DMA((2, groups, 2)),
            pltpu.SemaphoreType.DMA((2,)),
        ],
        compiler_params=pltpu.CompilerParams(collective_id=0, has_side_effects=True),
        name="reduce_shift",
    )(lengths, heads, weight, queries, new_kv, cache_kv, residual)


def on_device(residual, queries, new_kv, cache_kv, lengths, out_weight):
    sections = lax.axis_size("section")
    heads_count = lax.axis_size("head")
    heads = attend(queries, new_kv, cache_kv, lengths)
    projected, moved = reduce_shift(
        lengths, heads, out_weight[0], queries, new_kv, cache_kv, residual, sections, heads_count
    )
    projected = projected.astype(jnp.float32).transpose(1, 0, 2)
    return (moved.astype(jnp.float32) + projected).astype(jnp.bfloat16)


def solution(mesh):
    placed = (
        P(("section", "head"), None, None),
        P(None, "section", "head"),
        P(None, None, "section", None),
        P(None, "section", None),
        P(),
        P("section", "head", None),
    )
    return jax.shard_map(
        on_device,
        mesh=mesh,
        in_specs=placed,
        out_specs=P(("section", "head"), None, None),
        check_vma=False,
    )
```

time: 92.2 us -> 89.7 us (0.973); the launches traced: 91 us -> 90.4 us
  local copies, waits for them, and re-layouts: 1.58 us -> 0 us
  other arithmetic: 2.13 us -> 3.18 us
    pallas_call x1 -> x0, local copies, waits for them, and re-layouts: 1.58 us -> none  [reduce_shift(): pl.pallas_call(functools.partial(reduce_kernel, sections, heads_count), o...]
    transpose x0 -> x1, other arithmetic: none -> 0.99 us  [on_device(): projected = projected.astype(jnp.float32).transpose(1, 0, 2)]
where the time goes in v2:
time: 89.7 us; the launch traced here: 90.4 us
  Pallas kernels  87.2 us (97%)
  other arithmetic  3.18 us (4%)
    pallas_call x1, Pallas kernels, reduce_shift(): pl.pallas_call(functools.partial(reduce_kernel, sections, heads_count), o...  81.8 us
    pallas_call x1, Pallas kernels, attend(): pl.pallas_call(attend_kernel, out_shape=jax.ShapeDtypeStruct((rows, width...  5.41 us
    convert_element_type x1, other arithmetic, on_device(): return (moved.astype(jnp.float32) + projected).astype(jnp.bfloat16)  2.19 us

profile of v2, /device:TPU:1, one launch (start us, length us, event | category | flops | bytes accessed | tf_op | source)
XLA Modules:
  0.0 90.4 jit_solution(6278115752291426023)
XLA Ops:
  0.0 5.4 %attend.1.heads_hbm = bf16[256,256]{1,0:T(8,128)(2,1)} custom-call(s32[48]{0:T(128)} %len_ref.3, bf16[2,256,256]{2,1,0:T(8,128)(2,1)} %q_hbm.3, bf16[2,2,256,1024]{3,2,1,0:T(8,128)(2,1)} %new_ref.3, bf16[2,1536,1024]{2,1,0:T(8,128)(2,1)} %cache_ref.3), custom_call_target="tpu_custom_call" | custom-call | tf_op jit(solution)/shard_map/attend/pallas_call | solution.py:107
  5.4 81.8 %reduce_shift.1 = (bf16[2,16,4096]{2,1,0:T(8,128)(2,1)}, bf16[16,2,4096]{2,1,0:T(2,128)(2,1)}) custom-call(s32[48]{0:T(128)} %len_ref.3, bf16[256,256]{1,0:T(8,128)(2,1)} %attend.1.heads_hbm, bf16[256,4096]{1,0:T(8,128)(2,1)} %bitcast.5, bf16[2,256,256]{2,1,0:T(8,128)(2,1)} %q_hbm.3, bf16[2,2,256,1024]{3,2,1,0:T(8,128)(2,1)} %new_ref.3, ...), custom_call_target="tpu_custom_call" | custom-call | tf_op jit(solution)/shard_map/reduce_shift/pallas_call | solution.py:400
  87.2 1.0 %transpose.9 = f32[2,16,4096]{2,1,0:T(8,128)S(1)} convert(bf16[2,16,4096]{2,1,0:T(8,128)(2,1)} %get-tuple-element.8) | non-fusion elementwise | flops 131072 | bytes 786432 | tf_op jit(solution)/shard_map/transpose | solution.py:440
  88.2 2.2 %fusion = bf16[16,2,4096]{2,1,0:T(2,128)(2,1)} fusion(f32[2,16,4096]{2,1,0:T(8,128)S(1)} %transpose.9, bf16[16,2,4096]{2,1,0:T(2,128)(2,1)} %get-tuple-element.7), kind=kLoop, calls=%fused_computation.1 | loop fusion | flops 393216 | bytes 1048576 | tf_op jit(solution)/shard_map/convert_element_type | solution.py:441

commit v3 on v2

v3 whole, which is shorter than its diff:
```python
import functools
import math

import jax
import jax.numpy as jnp
from jax import lax
from jax.experimental import pallas as pl
from jax.experimental.pallas import tpu as pltpu
from jax.sharding import PartitionSpec as P

HD = 128
NEG = -1e30
SCALE = math.log2(math.e) / math.sqrt(HD)
SPLIT = 4
SKEW = (0, 0, 0, 0, 4, 4, 5, 5)
MESH = pl.DeviceIdType.MESH


def reduce_kernel(
    sections,
    heads_count,
    len_ref,
    q_hbm,
    new_ref,
    cache_ref,
    w_hbm,
    res_ref,
    out_ref,
    q_ref,
    kv,
    w_ref,
    mixed,
    part,
    buf,
    land,
    moved,
    summed,
    isem,
    wsem,
    ssem,
    rsem,
    zssem,
    zrsem,
    xsem,
):
    ny = heads_count // 2
    hops = ny - 1
    pairs = ny // 2
    groups = buf.shape[2]
    ticks, rows, width = q_ref.shape
    here = width // HD
    chunk = buf.shape[3]
    wide = buf.shape[4]
    own = chunk // 2
    half = w_ref.shape[1] // 2
    cached = cache_ref.shape[1]
    section = lax.axis_index("section")
    head = lax.axis_index("head")
    y = head // 2
    z = head % 2
    after = lax.rem(section + 1, sections)
    prior = lax.rem(section + sections - 1, sections)
    ring = (lax.rem(head + 2, heads_count), lax.rem(head + heads_count - 2, heads_count))
    column = pl.multiple_of((head // 2) * HD, HD)

    def column_of(d, g):
        return d * half + (g % SPLIT) * wide

    def w_copy(d, g):
        at = column_of(d, g)
        return pltpu.make_async_copy(
            w_hbm.at[:, at:at + wide], w_ref.at[:, at:at + wide], wsem.at[d, g]
        )

    def fresh_copy(t, i):
        at = t * (rows + cached)
        return pltpu.make_async_copy(
            new_ref.at[t, i, :, pl.ds(column, HD)],
            kv.at[i, at:at + rows, :],
            isem.at[1 + t, i],
        )

    def cache_copy(i):
        return pltpu.make_async_copy(
            cache_ref.at[i, :, pl.ds(column, HD)],
            kv.at[i, rows:rows + cached, :],
            isem.at[3, i],
        )

    q_copy = pltpu.make_async_copy(q_hbm, q_ref, isem.at[0, 0])
    q_copy.start()
    for i in range(2):
        fresh_copy(0, i).start()
        cache_copy(i).start()
    for g in range(SPLIT):
        for d in range(2):
            w_copy(d, g).start()
    for i in range(2):
        fresh_copy(1, i).start()

    barrier = pltpu.get_barrier_semaphore()
    for near in ring:
        pl.semaphore_signal(barrier, inc=1, device_id=(section, near), device_id_type=MESH)
    for other in range(2):
        for where in (after, prior):
            pl.semaphore_signal(
                barrier, inc=1, device_id=(where, 2 * y + other), device_id_type=MESH
            )

    def chunk_at(d, step):
        if d == 0:
            return lax.rem(y + 2 * ny - 1 - step, ny)
        return lax.rem(y + 1 + step, ny)

    def rows_of(c):
        return pl.ds(pl.multiple_of(c * chunk, chunk), chunk)

    def ring_copy(step, d, g):
        return pltpu.make_async_remote_copy(
            src_ref=buf.at[step, d, g],
            dst_ref=buf.at[step + 1, d, g],
            send_sem=ssem.at[step, d, g],
            recv_sem=rsem.at[step, d, g],
            device_id=(section, ring[d]),
            device_id_type=MESH,
        )

    def out_copy(d, g, target, source):
        return pltpu.make_async_remote_copy(
            src_ref=buf.at[hops, d, g, pl.ds(target * own, own), :],
            dst_ref=land.at[source, d, g],
            send_sem=zssem.at[d, g, target],
            recv_sem=zrsem.at[d, g, source],
            device_id=(after, 2 * y + target),
            device_id_type=MESH,
        )

    length = len_ref[section]

    def pair_of(p):
        return chunk_at(0, p), jnp.where(p == pairs - 1, y, chunk_at(1, p))

    def attend(t, p):
        pair = pair_of(p)
        q = jnp.concatenate(
            [q_ref[t, rows_of(c), h * HD:(h + 1) * HD] for h in range(here) for c in pair], axis=0
        )
        base = lax.broadcasted_iota(jnp.int32, (chunk, 1), 0)
        place = jnp.concatenate([base + c * chunk for h in range(here) for c in pair], axis=0)

        def scores(first, count):
            return lax.dot_general(
                q,
                kv[0, first:first + count, :],
                (((1,), (1,)), ((), ())),
                preferred_element_type=jnp.float32,
            )

        local = lax.broadcasted_iota(jnp.int32, (chunk * 2 * here, rows), 1)
        held = lax.broadcasted_iota(jnp.int32, (1, cached), 1)
        blocks = []
        first_block = scores(0, rows)
        blocks.append(jnp.where(local <= place, first_block, NEG) if t == 0 else first_block)
        blocks.append(jnp.where(held < length, scores(rows, cached), NEG))
        if t == 1:
            blocks.append(jnp.where(local <= place, scores(rows + cached, rows), NEG))
        s = jnp.concatenate(blocks, axis=1)
        m = jnp.max(s, axis=1, keepdims=True)
        w = jnp.exp2((s - m) * SCALE)
        total = jnp.sum(w, axis=1, keepdims=True)
        o = jnp.dot(
            w.astype(jnp.bfloat16), kv[1, 0:s.shape[1], :], preferred_element_type=jnp.float32
        )
        o = (o / total).astype(jnp.bfloat16)
        for h in range(here):
            mixed[:, h * HD:(h + 1) * HD] = o[2 * chunk * h:2 * chunk * (h + 1)]

    def project(t, p, d, g):
        pair = pair_of(p)
        at = column_of(d, g)
        block = jnp.dot(
            mixed[...], w_ref[:, at:at + wide], preferred_element_type=jnp.float32
        ).astype(jnp.bfloat16)
        for i in range(2):
            part[t, rows_of(pair[i]), at:at + wide] = block[i * chunk:(i + 1) * chunk]
        return block

    q_copy.wait()
    for i in range(2):
        fresh_copy(0, i).wait()
        cache_copy(i).wait()
    attend(0, 0)
    for g in range(SPLIT):
        for d in range(2):
            w_copy(d, g).wait()
            buf[0, d, g] = project(0, 0, d, g)[d * chunk:(d + 1) * chunk]
        if g == 0:
            pl.semaphore_wait(barrier, 6)
        for d in range(2):
            ring_copy(0, d, g).start()
    res_copy = pltpu.make_async_remote_copy(
        src_ref=res_ref,
        dst_ref=moved,
        send_sem=xsem.at[0],
        recv_sem=xsem.at[1],
        device_id=(after, head),
        device_id_type=MESH,
    )
    res_copy.start()
    for i in range(2):
        fresh_copy(1, i).wait()

    def attend_next(k):
        for t in range(ticks):
            @pl.when(jnp.logical_and(k >= t * pairs, k < (t + 1) * pairs))
            def _(t=t):
                attend(t, k - t * pairs)

    def project_next(k, d):
        for t in range(ticks):
            @pl.when(jnp.logical_and(k >= t * pairs, k < (t + 1) * pairs))
            def _(t=t):
                for g in range(SPLIT):
                    project(t, k - t * pairs, d, g)

    attend_next(1)
    for d in range(2):
        project_next(1, d)

    def slot(now, carry):
        for g in range(SPLIT, groups):
            @pl.when(now == SKEW[g])
            def _(g=g):
                for d in range(2):
                    at = column_of(d, g)
                    buf[0, d, g] = part[1, rows_of(chunk_at(d, 0)), at:at + wide]
                    ring_copy(0, d, g).start()

        for g in range(groups):
            t = g // SPLIT
            step = now - SKEW[g]

            @pl.when(jnp.logical_and(step >= 1, step <= hops))
            def _(g=g, t=t, step=step):
                for d in range(2):
                    ring_copy(step - 1, d, g).wait_recv()
                    at = column_of(d, g)
                    mine = part[t, rows_of(chunk_at(d, step)), at:at + wide]
                    buf[step, d, g] = (
                        buf[step, d, g].astype(jnp.float32) + mine.astype(jnp.float32)
                    ).astype(jnp.bfloat16)

                    @pl.when(step < hops)
                    def _():
                        ring_copy(step, d, g).start()

                    @pl.when(step == hops)
                    def _():
                        for target in range(2):
                            out_copy(d, g, target, z).start()

            if g == 1:
                attend_next(now + 1)
            if g == 2 or g == 3:
                project_next(now + 1, g - 2)

        return carry

    lax.fori_loop(1, hops + 1 + max(SKEW), slot, 0)

    res_copy.wait_recv()
    for g in range(groups):
        for d in range(2):
            for other in range(2):
                out_copy(d, g, other, other).wait_recv()
            at = column_of(d, g)
            summed[:, g // SPLIT, at:at + wide] = land[0, d, g].astype(jnp.float32) + land[
                1, d, g
            ].astype(jnp.float32)
            if g >= groups - SPLIT:
                out_ref[:, :, at:at + wide] = (
                    summed[:, :, at:at + wide] + moved[:, :, at:at + wide].astype(jnp.float32)
                ).astype(jnp.bfloat16)
    for d in range(2):
        for g in range(groups):
            for other in range(2):
                out_copy(d, g, other, other).wait_send()

            def drain(step, carry, d=d, g=g):
                ring_copy(step, d, g).wait_send()
                return carry

            lax.fori_loop(0, hops, drain, 0)
    res_copy.wait_send()


def on_device(residual, queries, new_kv, cache_kv, lengths, out_weight):
    sections = lax.axis_size("section")
    heads_count = lax.axis_size("head")
    weight = out_weight[0]
    ticks, rows, width = queries.shape
    depth = weight.shape[1]
    ny = heads_count // 2
    hops = ny - 1
    groups = ticks * SPLIT
    chunk = rows // ny
    wide = depth // 2 // SPLIT
    keys = cache_kv.shape[1] + ticks * rows
    any_space = pl.BlockSpec(memory_space=pl.ANY)
    return pl.pallas_call(
        functools.partial(reduce_kernel, sections, heads_count),
        out_shape=jax.ShapeDtypeStruct(residual.shape, jnp.bfloat16),
        in_specs=[pl.BlockSpec(memory_space=pltpu.SMEM)] + [any_space] * 5,
        out_specs=pl.BlockSpec(memory_space=pltpu.VMEM),
        scratch_shapes=[
            pltpu.VMEM((ticks, rows, width), jnp.bfloat16),
            pltpu.VMEM((2, keys, HD), jnp.bfloat16),
            pltpu.VMEM(weight.shape, jnp.bfloat16),
            pltpu.VMEM((2 * chunk, width), jnp.bfloat16),
            pltpu.VMEM((ticks, rows, depth), jnp.bfloat16),
            pltpu.VMEM((hops + 1, 2, groups, chunk, wide), jnp.bfloat16),
            pltpu.VMEM((2, 2, groups, chunk // 2, wide), jnp.bfloat16),
            pltpu.VMEM(residual.shape, jnp.bfloat16),
            pltpu.VMEM(residual.shape, jnp.float32),
            pltpu.SemaphoreType.DMA((4, 2)),
            pltpu.SemaphoreType.DMA((2, SPLIT)),
            pltpu.SemaphoreType.DMA((hops, 2, groups)),
            pltpu.SemaphoreType.DMA((hops, 2, groups)),
            pltpu.SemaphoreType.DMA((2, groups, 2)),
            pltpu.SemaphoreType.DMA((2, groups, 2)),
            pltpu.SemaphoreType.DMA((2,)),
        ],
        compiler_params=pltpu.CompilerParams(collective_id=0, has_side_effects=True),
        name="attend_reduce_shift",
    )(lengths, queries, new_kv, cache_kv, weight, residual)


def solution(mesh):
    placed = (
        P(("section", "head"), None, None),
        P(None, "section", "head"),
        P(None, None, "section", None),
        P(None, "section", None),
        P(),
        P("section", "head", None),
    )
    return jax.shard_map(
        on_device,
        mesh=mesh,
        in_specs=placed,
        out_specs=P(("section", "head"), None, None),
        check_vma=False,
    )
```

time: 89.7 us -> 81.8 us (0.912)
  Pallas kernels: 87.2 us -> 79.8 us
  other arithmetic: 3.18 us -> 0 us
  local copies, waits for them, and re-layouts: 0 us -> 1.85 us
    pallas_call x2 -> x1, Pallas kernels: 87.2 us -> 79.8 us  [on_device(): pl.pallas_call(functools.partial(reduce_kernel, sections, heads_count), o...]
    convert_element_type x1 -> x0, other arithmetic: 2.19 us -> none  [on_device(): return (moved.astype(jnp.float32) + projected).astype(jnp.bfloat16)]
    unnamed x0 -> x1, local copies, waits for them, and re-layouts: none -> 1.85 us
    transpose x1 -> x0, other arithmetic: 0.99 us -> none  [on_device(): projected = projected.astype(jnp.float32).transpose(1, 0, 2)]
where the time goes in v3:
time: 81.8 us; the launch traced here: 81.6 us
  Pallas kernels  79.8 us (98%)
  local copies, waits for them, and re-layouts  1.85 us (2%)
    pallas_call x1, Pallas kernels, on_device(): pl.pallas_call(functools.partial(reduce_kernel, sections, heads_count), o...  79.8 us
    unnamed x1, local copies, waits for them, and re-layouts  1.85 us

profile of v3, /device:TPU:1, one launch (start us, length us, event | category | flops | bytes accessed | tf_op | source)
XLA Modules:
  0.0 81.6 jit_solution(8637897399392113461)
XLA Ops:
  0.0 79.8 %attend_reduce_shift.1 = bf16[16,2,4096]{2,1,0:T(2,128)(2,1)} custom-call(s32[48]{0:T(128)} %len_ref.1, bf16[2,256,256]{2,1,0:T(8,128)(2,1)} %q_hbm.1, bf16[2,2,256,1024]{3,2,1,0:T(8,128)(2,1)} %new_ref.1, bf16[2,1536,1024]{2,1,0:T(8,128)(2,1)} %cache_ref.1, bf16[256,4096]{1,0:T(8,128)(2,1)} %bitcast.1, bf16[16,2,4096]{2,1,0:T(2,128)(2,1)} %res_ref.1), custom_call_target="tpu_custom_call" | custom-call | tf_op jit(solution)/shard_map/attend_reduce_shift/pallas_call | solution.py:310
  79.8 1.9 %copy.8 = bf16[16,2,4096]{2,1,0:T(2,128)(2,1)} copy(bf16[16,2,4096]{2,1,0:T(2,128)(2,1)} %attend_reduce_shift.1) | data formatting | bytes 524288

commit v4 on v3

--- a/solution.py
+++ b/solution.py
@@ -12,7 +12,8 @@
 NEG = -1e30
 SCALE = math.log2(math.e) / math.sqrt(HD)
 SPLIT = 4
-SKEW = (0, 0, 0, 0, 4, 4, 5, 5)
+LAG = 3
+SKEW = (0,) * SPLIT + (LAG,) * SPLIT
 MESH = pl.DeviceIdType.MESH
 
 
@@ -140,7 +141,7 @@
     def pair_of(p):
         return chunk_at(0, p), jnp.where(p == pairs - 1, y, chunk_at(1, p))
 
-    def attend(t, p):
+    def attend(t, p, before_values=None):
         pair = pair_of(p)
         q = jnp.concatenate(
             [q_ref[t, rows_of(c), h * HD:(h + 1) * HD] for h in range(here) for c in pair], axis=0
@@ -168,28 +169,33 @@
         m = jnp.max(s, axis=1, keepdims=True)
         w = jnp.exp2((s - m) * SCALE)
         total = jnp.sum(w, axis=1, keepdims=True)
+        if before_values is not None:
+            before_values()
         o = jnp.dot(
             w.astype(jnp.bfloat16), kv[1, 0:s.shape[1], :], preferred_element_type=jnp.float32
         )
         o = (o / total).astype(jnp.bfloat16)
         for h in range(here):
-            mixed[:, h * HD:(h + 1) * HD] = o[2 * chunk * h:2 * chunk * (h + 1)]
+            mixed[t, :, h * HD:(h + 1) * HD] = o[2 * chunk * h:2 * chunk * (h + 1)]
 
     def project(t, p, d, g):
         pair = pair_of(p)
         at = column_of(d, g)
         block = jnp.dot(
-            mixed[...], w_ref[:, at:at + wide], preferred_element_type=jnp.float32
+            mixed[t], w_ref[:, at:at + wide], preferred_element_type=jnp.float32
         ).astype(jnp.bfloat16)
         for i in range(2):
             part[t, rows_of(pair[i]), at:at + wide] = block[i * chunk:(i + 1) * chunk]
         return block
 
+    def values_here():
+        fresh_copy(0, 1).wait()
+        cache_copy(1).wait()
+
     q_copy.wait()
-    for i in range(2):
-        fresh_copy(0, i).wait()
-        cache_copy(i).wait()
-    attend(0, 0)
+    fresh_copy(0, 0).wait()
+    cache_copy(0).wait()
+    attend(0, 0, values_here)
     for g in range(SPLIT):
         for d in range(2):
             w_copy(d, g).wait()
@@ -212,16 +218,16 @@
 
     def attend_next(k):
         for t in range(ticks):
-            @pl.when(jnp.logical_and(k >= t * pairs, k < (t + 1) * pairs))
+            @pl.when(jnp.logical_and(k >= t * LAG, k < t * LAG + pairs))
             def _(t=t):
-                attend(t, k - t * pairs)
+                attend(t, k - t * LAG)
 
     def project_next(k, d):
         for t in range(ticks):
-            @pl.when(jnp.logical_and(k >= t * pairs, k < (t + 1) * pairs))
+            @pl.when(jnp.logical_and(k >= t * LAG, k < t * LAG + pairs))
             def _(t=t):
                 for g in range(SPLIT):
-                    project(t, k - t * pairs, d, g)
+                    project(t, k - t * LAG, d, g)
 
     attend_next(1)
     for d in range(2):
@@ -259,10 +265,12 @@
                         for target in range(2):
                             out_copy(d, g, target, z).start()
 
-            if g == 1:
+            if g == SPLIT // 4:
                 attend_next(now + 1)
-            if g == 2 or g == 3:
-                project_next(now + 1, g - 2)
+            if g == SPLIT // 2:
+                project_next(now + 1, 0)
+            if g == SPLIT - 1:
+                project_next(now + 1, 1)
 
         return carry
 
@@ -294,6 +302,12 @@
     res_copy.wait_send()
 
 
+def hand_over_kernel(in_ref, out_ref, sem):
+    copy = pltpu.make_async_copy(in_ref, out_ref, sem)
+    copy.start()
+    copy.wait()
+
+
 def on_device(residual, queries, new_kv, cache_kv, lengths, out_weight):
     sections = lax.axis_size("section")
     heads_count = lax.axis_size("head")
@@ -307,16 +321,17 @@
     wide = depth // 2 // SPLIT
     keys = cache_kv.shape[1] + ticks * rows
     any_space = pl.BlockSpec(memory_space=pl.ANY)
-    return pl.pallas_call(
+    result = pl.pallas_call(
         functools.partial(reduce_kernel, sections, heads_count),
         out_shape=jax.ShapeDtypeStruct(residual.shape, jnp.bfloat16),
-        in_specs=[pl.BlockSpec(memory_space=pltpu.SMEM)] + [any_space] * 5,
+        in_specs=[pl.BlockSpec(memory_space=pltpu.SMEM)]
+        + [pl.BlockSpec(memory_space=pltpu.HBM)] * 5,
         out_specs=pl.BlockSpec(memory_space=pltpu.VMEM),
         scratch_shapes=[
             pltpu.VMEM((ticks, rows, width), jnp.bfloat16),
             pltpu.VMEM((2, keys, HD), jnp.bfloat16),
             pltpu.VMEM(weight.shape, jnp.bfloat16),
-            pltpu.VMEM((2 * chunk, width), jnp.bfloat16),
+            pltpu.VMEM((ticks, 2 * chunk, width), jnp.bfloat16),
             pltpu.VMEM((ticks, rows, depth), jnp.bfloat16),
             pltpu.VMEM((hops + 1, 2, groups, chunk, wide), jnp.bfloat16),
             pltpu.VMEM((2, 2, groups, chunk // 2, wide), jnp.bfloat16),
@@ -330,9 +345,23 @@
             pltpu.SemaphoreType.DMA((2, groups, 2)),
             pltpu.SemaphoreType.DMA((2,)),
         ],
-        compiler_params=pltpu.CompilerParams(collective_id=0, has_side_effects=True),
+        compiler_params=pltpu.CompilerParams(collective_id=0, has_side_effects=True, vmem_limit_bytes=24 * 1024 * 1024),
         name="attend_reduce_shift",
-    )(lengths, queries, new_kv, cache_kv, weight, residual)
+    )(
+        *(
+            pltpu.with_memory_space_constraint(a, pltpu.HBM)
+            for a in (lengths, queries, new_kv, cache_kv, weight, residual)
+        ),
+    )
+    return pl.pallas_call(
+        hand_over_kernel,
+        out_shape=jax.ShapeDtypeStruct(residual.shape, jnp.bfloat16),
+        in_specs=[any_space],
+        out_specs=any_space,
+        scratch_shapes=[pltpu.SemaphoreType.DMA],
+        compiler_params=pltpu.CompilerParams(vmem_limit_bytes=1024 * 1024),
+        name="hand_over",
+    )(result)
 
 
 def solution(mesh):

time: 81.8 us -> 79.1 us (0.967)
  local copies, waits for them, and re-layouts: 1.85 us -> 0 us
    unnamed x1 -> x0, local copies, waits for them, and re-layouts: 1.85 us -> none
    pallas_call x1, Pallas kernels: 79.8 us -> 78.3 us  [on_device(): pl.pallas_call(functools.partial(reduce_kernel, sections, heads_count), o...]
where the time goes in v4:
time: 79.1 us; the launch traced here: 79 us
  Pallas kernels  79 us (100%)
    pallas_call x1, Pallas kernels, on_device(): pl.pallas_call(functools.partial(reduce_kernel, sections, heads_count), o...  78.3 us

profile of v4, /device:TPU:1, one launch (start us, length us, event | category | flops | bytes accessed | tf_op | source)
XLA Modules:
  0.0 79.0 jit_solution(2439641586934608859)
XLA Ops:
  0.0 78.3 %attend_reduce_shift.1.in_ref = bf16[16,2,4096]{2,1,0:T(2,128)(2,1)S(1)} custom-call(s32[48]{0:T(128)} %len_ref.1, bf16[2,256,256]{2,1,0:T(8,128)(2,1)} %q_hbm.1, bf16[2,2,256,1024]{3,2,1,0:T(8,128)(2,1)} %new_ref.1, bf16[2,1536,1024]{2,1,0:T(8,128)(2,1)} %cache_ref.1, bf16[256,4096]{1,0:T(8,128)(2,1)} %bitcast.1, bf16[16,2,4096]{2,1,0:T(2,128)(2,1)} %res_ref.1), custom_call_target="tpu_custom_call" | custom-call | tf_op jit(solution)/shard_map/attend_reduce_shift/pallas_call | solution.py:324
  78.3 0.7 hand_over.1

commit v5 on v4

--- a/solution.py
+++ b/solution.py
@@ -13,7 +13,7 @@
 SCALE = math.log2(math.e) / math.sqrt(HD)
 SPLIT = 4
 LAG = 3
-SKEW = (0,) * SPLIT + (LAG,) * SPLIT
+SKEW = (0,) * SPLIT + (LAG,) * (SPLIT // 2) + (LAG + 1,) * (SPLIT // 2)
 MESH = pl.DeviceIdType.MESH
 
 

time: 79.1 us -> 79.5 us (level)
  no operation moved by 1% of the time
where the time goes in v5:
time: 79.5 us; the launch traced here: 79.4 us
  Pallas kernels  79.4 us (100%)
    pallas_call x1, Pallas kernels, on_device(): pl.pallas_call(functools.partial(reduce_kernel, sections, heads_count), o...  78.7 us

profile of v5, /device:TPU:1, one launch (start us, length us, event | category | flops | bytes accessed | tf_op | source)
XLA Modules:
  0.0 79.4 jit_solution(10001921414825855073)
XLA Ops:
  0.0 78.7 %attend_reduce_shift.1.in_ref = bf16[16,2,4096]{2,1,0:T(2,128)(2,1)S(1)} custom-call(s32[48]{0:T(128)} %len_ref.1, bf16[2,256,256]{2,1,0:T(8,128)(2,1)} %q_hbm.1, bf16[2,2,256,1024]{3,2,1,0:T(8,128)(2,1)} %new_ref.1, bf16[2,1536,1024]{2,1,0:T(8,128)(2,1)} %cache_ref.1, bf16[256,4096]{1,0:T(8,128)(2,1)} %bitcast.1, bf16[16,2,4096]{2,1,0:T(2,128)(2,1)} %res_ref.1), custom_call_target="tpu_custom_call" | custom-call | tf_op jit(solution)/shard_map/attend_reduce_shift/pallas_call | solution.py:324
  78.7 0.7 hand_over.1
